TPU v7x, 256 devices: a whole 4x4x8 slice. The times are simulated.
256 devices in a mesh: pair: 64 (over x, y_hi, z), tm: 4 (over y_lo, core).
Axes of the slice: x: 4, y: 4 (y_hi: 2, y_lo: 2; y = y_hi * 2 + y_lo), z: 8, core: 2. Of those that a mesh axis runs over, the one named last changes fastest.
Arguments:
- history: float32 [8192, 32768], P('tm', 'pair'), may hold values from -6 to 6
- round_index: int32 [1], replicated, may hold values from 0 to 126
Outputs:
- rotated: float32 [8192, 32768], P('tm', 'pair')
Inputs may be any that keep to these rules, and one draw needn't show every extreme that they name: `round_index`: the same value on every device.
All inputs are finite; a program needn't handle non-finite values.
Results may differ from a plain program's by a relative error of at most 0.0003.
Values sent between devices are 32-bit elements; how exact they have to be, the bound alone decides.
A program may use at most 64 MiB of HBM per device.

v0:
```python
import functools

import jax
import jax.numpy as jnp
from jax import lax
from jax.experimental import pallas as pl
from jax.experimental.pallas import tpu as pltpu
from jax.sharding import PartitionSpec as P

STEPS = 4
EPS = 1e-06
T = 128
BLOCKS = [(i, j) for i in range(4) for j in range(i, 4)]
OWN = [BLOCKS[:5], BLOCKS[5:]]
CHUNKS = 8
MESH = pl.DeviceIdType.MESH
F32 = jnp.float32
BF16 = jnp.bfloat16


def split(value):
    high = value.astype(BF16)
    return high, (value - high.astype(F32)).astype(BF16)


def dot(a, b):
    return jnp.dot(a, b, preferred_element_type=F32)


def dot_t(a, b):
    return lax.dot_general(a, b, (((0,), (0,)), ((), ())), preferred_element_type=F32)


def kernel(
    round_ref, hist, top, bot,
    stage, bh, bl, hh, mm, part, fin, recv_a, recv_b, x, xh, xl, ph, pm, out_r, out_l,
    load_sem, a_sem, b_sem, c_sem, r_send, l_send, r_recv, l_recv,
):
    rows, cols = hist.shape
    width = cols // 2
    step_rows = rows // CHUNKS
    pair_count = lax.axis_size("pair")
    pos = lax.axis_index("pair")
    tm = lax.axis_index("tm")
    core = lax.rem(tm, 2)
    sibling = {"tm": tm + 1 - 2 * core}
    across = {"tm": lax.rem(tm + 2, 4)}
    right = {"pair": jnp.minimum(pos + 1, pair_count - 1)}
    left = {"pair": jnp.maximum(pos - 1, 0)}
    has_right = pos < pair_count - 1
    has_left = pos > 0

    def load(i):
        rs = pl.ds(i * step_rows, step_rows)
        return pltpu.make_async_copy(hist.at[rs], stage.at[rs], load_sem.at[i])

    for i in range(CHUNKS):
        load(i).start()

    barrier = pltpu.get_barrier_semaphore()
    for target in (sibling, across):
        pl.semaphore_signal(barrier, inc=1, device_id=target, device_id_type=MESH)

    @pl.when(has_right)
    def _():
        pl.semaphore_signal(barrier, inc=1, device_id=right, device_id_type=MESH)

    @pl.when(has_left)
    def _():
        pl.semaphore_signal(barrier, inc=1, device_id=left, device_id_type=MESH)

    for i in range(CHUNKS):
        load(i).wait()
        rs = pl.ds(i * step_rows, step_rows)
        h, l = split(stage[rs, :])
        bh[rs, :] = h
        bl[rs, :] = l
        g_top = dot_t(h[:, :width], h)
        g_bot = dot_t(h[:, width:], h[:, width:])
        m_new = dot_t(h, l)
        if i == 0:
            hh[:width, :] = g_top
            hh[width:, width:] = g_bot
            mm[...] = m_new
        else:
            hh[:width, :] += g_top
            hh[width:, width:] += g_bot
            mm[...] += m_new

    for k, (i, j) in enumerate(BLOCKS):
        si, sj = pl.ds(i * T, T), pl.ds(j * T, T)
        part[k] = hh[si, sj] + (mm[si, sj] + mm[sj, si].T)

    peers = 2 + has_right.astype(jnp.int32) + has_left.astype(jnp.int32)
    pl.semaphore_wait(barrier, peers)

    half = len(BLOCKS) // 2
    mine, other = core * half, (1 - core) * half

    swap = pltpu.make_async_remote_copy(
        part.at[pl.ds(other, half)], recv_a, a_sem.at[0], a_sem.at[1],
        device_id=sibling, device_id_type=MESH,
    )
    swap.start()

    def cross(k):
        return pltpu.make_async_remote_copy(
            part.at[mine + k], recv_b.at[k], b_sem.at[0, k], b_sem.at[1, k],
            device_id=across, device_id_type=MESH,
        )

    def share(k, offset):
        return pltpu.make_async_remote_copy(
            fin.at[offset + k], fin.at[offset + k], c_sem.at[0, k], c_sem.at[1, k],
            device_id=sibling, device_id_type=MESH,
        )

    swap.wait()
    for k in range(half):
        part[mine + k] = part[mine + k] + recv_a[k]
        cross(k).start()
    for k in range(half):
        cross(k).wait_recv()
        fin[mine + k] = part[mine + k] + recv_b[k]
        share(k, mine).start()
    for k in range(half):
        share(k, other).wait_recv()

    cycle = 2 * pair_count - 1
    now = round_ref[0]

    def wrap(value):
        return lax.rem(lax.rem(value, cycle) + cycle, cycle)

    top_id = jnp.where(pos == 0, 0, 1 + wrap(pos - 1 - now))
    bottom_id = 1 + wrap(2 * pair_count - 2 - pos - now)
    sign = jnp.where(top_id < bottom_id, 1.0, -1.0).astype(F32)
    row_at = lax.broadcasted_iota(jnp.int32, (T, T), 0)
    col_at = lax.broadcasted_iota(jnp.int32, (T, T), 1)
    on_diag = row_at == col_at
    within = jnp.where(row_at < col_at, 1.0, jnp.where(on_diag, 0.0, -1.0)).astype(F32)
    along, down = [], []
    for i in range(4):
        d = jnp.where(on_diag, fin[BLOCKS.index((i, i))], 0.0)
        along.append(jnp.sum(d, axis=0, keepdims=True))
        down.append(jnp.sum(d, axis=1, keepdims=True))
    total = jnp.zeros((T, T), F32)
    for k, (i, j) in enumerate(BLOCKS):
        si, sj = pl.ds(i * T, T), pl.ds(j * T, T)
        value = fin[k] / (down[i] + along[j] + EPS)
        if i == j:
            value = value * within
            total = total + value * value
            x[si, sj] = value
        else:
            if i < 2 <= j:
                value = value * sign
            total = total + 2.0 * (value * value)
            x[si, sj] = value
            x[sj, si] = -value.T
    scale = 1.0 / jnp.sqrt(1.0 + jnp.sum(total, keepdims=True))
    wide_eye = (
        lax.broadcasted_iota(jnp.int32, (cols, cols), 0)
        == lax.broadcasted_iota(jnp.int32, (cols, cols), 1)
    )
    start = (x[...] + jnp.where(wide_eye, 1.0, 0.0)) * scale
    x[...] = start
    h, l = split(start)
    xh[...] = h
    xl[...] = l

    def polar(step, carry):
        h, l = xh[...], xl[...]
        square = dot_t(h, h) + (dot_t(h, l) + dot_t(l, h))
        p = jnp.where(wide_eye, 1.5, 0.0) - 0.5 * square
        p_h, p_l = split(p)
        ph[...] = p_h
        pm[...] = p_l
        new = dot(xh[...], ph[...]) + (dot(xh[...], pm[...]) + dot(xl[...], ph[...]))
        n_h, n_l = split(new)
        xh[...] = n_h
        xl[...] = n_l
        return carry

    lax.fori_loop(0, STEPS, polar, 0)

    @pl.when(pos == 0)
    def _():
        ph[:, :width] = xh[:, width:]
        ph[:, width:] = xh[:, :width]
        pm[:, :width] = xl[:, width:]
        pm[:, width:] = xl[:, :width]

    @pl.when(pos > 0)
    def _():
        ph[...] = xh[...]
        pm[...] = xl[...]

    def to_right(i):
        rs = pl.ds(i * step_rows, step_rows)
        return pltpu.make_async_remote_copy(
            out_r.at[rs], top.at[rs], r_send.at[i], r_recv.at[i],
            device_id=right, device_id_type=MESH,
        )

    def to_left(i):
        rs = pl.ds(i * step_rows, step_rows)
        return pltpu.make_async_remote_copy(
            out_l.at[rs], bot.at[rs], l_send.at[i], l_recv.at[i],
            device_id=left, device_id_type=MESH,
        )

    def rotate(i, carry):
        rs = pl.ds(pl.multiple_of(i * step_rows, step_rows), step_rows)
        h, l = bh[rs, :], bl[rs, :]
        r = dot(h, ph[...]) + (dot(h, pm[...]) + dot(l, ph[...]))
        out_r[rs, :] = r[:, :width]
        out_l[rs, :] = r[:, width:]

        @pl.when(has_right)
        def _():
            to_right(i).start()

        @pl.when(jnp.logical_not(has_right))
        def _():
            pltpu.make_async_copy(out_r.at[rs], bot.at[rs], l_recv.at[i]).start()

        @pl.when(has_left)
        def _():
            to_left(i).start()

        @pl.when(jnp.logical_not(has_left))
        def _():
            pltpu.make_async_copy(out_l.at[rs], top.at[rs], r_recv.at[i]).start()

        return carry

    lax.fori_loop(0, CHUNKS, rotate, 0)

    for k in range(half):
        cross(k).wait_send()
        share(k, mine).wait_send()

    def finish(i, carry):
        @pl.when(has_right)
        def _():
            to_right(i).wait_send()

        @pl.when(has_left)
        def _():
            to_left(i).wait_send()

        to_right(i).wait_recv()
        to_left(i).wait_recv()
        return carry

    lax.fori_loop(0, CHUNKS, finish, 0)


def shards(history, round_index):
    rows, cols = history.shape
    width = cols // 2
    half = len(BLOCKS) // 2
    vmem = pltpu.VMEM
    dma = pltpu.SemaphoreType.DMA
    top, bot = pl.pallas_call(
        kernel,
        out_shape=[jax.ShapeDtypeStruct((rows, width), F32)] * 2,
        in_specs=[
            pl.BlockSpec(memory_space=pltpu.SMEM),
            pl.BlockSpec(memory_space=pl.ANY),
        ],
        out_specs=[pl.BlockSpec(memory_space=pl.ANY)] * 2,
        scratch_shapes=[
            vmem((rows, cols), F32),
            vmem((rows, cols), BF16),
            vmem((rows, cols), BF16),
            vmem((cols, cols), F32),
            vmem((cols, cols), F32),
            vmem((2 * half, T, T), F32),
            vmem((2 * half, T, T), F32),
            vmem((half, T, T), F32),
            vmem((half, T, T), F32),
            vmem((cols, cols), F32),
            vmem((cols, cols), BF16),
            vmem((cols, cols), BF16),
            vmem((cols, cols), BF16),
            vmem((cols, cols), BF16),
            vmem((rows, width), F32),
            vmem((rows, width), F32),
            dma((CHUNKS,)),
            dma((2,)),
            dma((2, half)),
            dma((2, half)),
            dma((CHUNKS,)),
            dma((CHUNKS,)),
            dma((CHUNKS,)),
            dma((CHUNKS,)),
        ],
        compiler_params=pltpu.CompilerParams(
            collective_id=0, has_side_effects=True, vmem_limit_bytes=48 * 1024 * 1024
        ),
        name="pairing_round",
    )(round_index, history)
    return jnp.concatenate([top, bot], axis=1)


def solution(mesh):
    in_specs = (P("tm", "pair"), P())
    out_specs = P("tm", "pair")
    return jax.shard_map(shards, mesh=mesh, in_specs=in_specs, out_specs=out_specs, check_vma=False)
```

profile of v0, /device:TPU:7, one launch (start us, length us, event | category | flops | bytes accessed | tf_op | source)
XLA Modules:
  0.0 85.0 jit_solution(3062721239442306308)
XLA Ops:
  0.7 81.7 %pairing_round.1 = (f32[2048,256]{1,0:T(8,128)S(1)}, f32[2048,256]{1,0:T(8,128)S(1)}) custom-call(s32[1]{0:T(128)S(6)} %copy.3.round_ref, f32[2048,512]{1,0:T(8,128)} %hist.1), custom_call_target="tpu_custom_call" | custom-call | tf_op jit(solution)/shard_map/pairing_round/pallas_call | solution.py:266
  82.4 2.7 %pad_maximum_fusion = f32[2048,512]{1,0:T(8,128)} fusion(f32[2048,256]{1,0:T(8,128)S(1)} %get-tuple-element.8, f32[2048,256]{1,0:T(8,128)S(1)} %get-tuple-element.7), kind=kLoop, calls=%fused_computation | loop fusion | flops 1048576 | bytes 8388608 | tf_op jit(solution)/shard_map/concatenate | solution.py:305
where the time goes:
time: 85.1 us; the launch traced here: 85 us
  Pallas kernels  81.7 us (96%)
  other arithmetic  2.67 us (3%)
    pallas_call x1, Pallas kernels, shards(): pl.pallas_call(kernel, out_shape=[jax.ShapeDtypeStruct((rows, width), F32...  81.7 us
    concatenate x1, other arithmetic, shards(): return jnp.concatenate([top, bot], axis=1)  2.67 us

commit v1 on v0

v1 whole, which is shorter than its diff:
```python
import functools

import jax
import jax.numpy as jnp
from jax import lax
from jax.experimental import pallas as pl
from jax.experimental.pallas import tpu as pltpu
from jax.sharding import PartitionSpec as P

STEPS = 4
EPS = 1e-06
T = 128
BLOCKS = [(0, 0), (0, 1), (2, 2), (2, 3), (0, 2), (0, 3), (1, 2), (1, 3)]
GROUPS = [(0, 2), (2, 2), (4, 2), (6, 2)]
CHUNKS = 8
PIECES = 4
MESH = pl.DeviceIdType.MESH
F32 = jnp.float32
BF16 = jnp.bfloat16


def split(value):
    high = value.astype(BF16)
    return high, (value - high.astype(F32)).astype(BF16)


def dot(a, b):
    return jnp.dot(a, b, preferred_element_type=F32)


def dot_nt(a, b):
    return lax.dot_general(a, b, (((1,), (1,)), ((), ())), preferred_element_type=F32)


def kernel(
    round_ref, hist, top, bot,
    stage, bh, bl, bt, part, fin, recv_a, recv_b, dv, x, xh, xl, ph, pm, out_r, out_l,
    load_sem, a_sem, b_sem, c_sem, d_sem, r_send, l_send, r_recv, l_recv,
):
    rows, cols = hist.shape
    width = cols // 2
    step_rows = rows // CHUNKS
    pair_count = lax.axis_size("pair")
    pos = lax.axis_index("pair")
    tm = lax.axis_index("tm")
    core = lax.rem(tm, 2)
    sibling = {"tm": tm + 1 - 2 * core}
    across = {"tm": lax.rem(tm + 2, 4)}
    right = {"pair": jnp.minimum(pos + 1, pair_count - 1)}
    left = {"pair": jnp.maximum(pos - 1, 0)}
    has_right = pos < pair_count - 1
    has_left = pos > 0

    def load(i):
        rs = pl.ds(i * step_rows, step_rows)
        return pltpu.make_async_copy(hist.at[rs], stage.at[rs], load_sem.at[i])

    for i in range(CHUNKS):
        load(i).start()

    barrier = pltpu.get_barrier_semaphore()
    for target in (sibling, across):
        pl.semaphore_signal(barrier, inc=1, device_id=target, device_id_type=MESH)

    @pl.when(has_right)
    def _():
        pl.semaphore_signal(barrier, inc=1, device_id=right, device_id_type=MESH)

    @pl.when(has_left)
    def _():
        pl.semaphore_signal(barrier, inc=1, device_id=left, device_id_type=MESH)

    lo, hi = pl.ds(0, width), pl.ds(width, width)
    first_high, first_low = None, None
    for i in range(CHUNKS):
        load(i).wait()
        rs = pl.ds(i * step_rows, step_rows)
        h, l = split(stage[rs, :])
        bh[rs, :] = h
        bl[rs, :] = l
        bt[:, rs] = h.T
        new_high = dot(bt[lo, rs], bh[rs, lo])
        new_low = dot(bt[lo, rs], bl[rs, lo])
        first_high = new_high if i == 0 else first_high + new_high
        first_low = new_low if i == 0 else first_low + new_low

    mine, other = pl.ds(core * (T // 2), T // 2), pl.ds((1 - core) * (T // 2), T // 2)

    def swap(g):
        group = pl.ds(*GROUPS[g])
        return pltpu.make_async_remote_copy(
            part.at[group, other], recv_a.at[group], a_sem.at[0, g], a_sem.at[1, g],
            device_id=sibling, device_id_type=MESH,
        )

    def cross(g):
        group = pl.ds(*GROUPS[g])
        return pltpu.make_async_remote_copy(
            part.at[group, mine], recv_b.at[group], b_sem.at[0, g], b_sem.at[1, g],
            device_id=across, device_id_type=MESH,
        )

    def share(g, rows_of):
        group = pl.ds(*GROUPS[g])
        return pltpu.make_async_remote_copy(
            fin.at[group, rows_of], fin.at[group, rows_of], c_sem.at[0, g], c_sem.at[1, g],
            device_id=sibling, device_id_type=MESH,
        )

    def send_on(g):
        swap(g).wait_recv()
        group = pl.ds(*GROUPS[g])
        part[group, mine] = part[group, mine] + recv_a[group]
        cross(g).start()

    row_at = lax.broadcasted_iota(jnp.int32, (T, T), 0)
    col_at = lax.broadcasted_iota(jnp.int32, (T, T), 1)
    on_diag = row_at == col_at
    upper, lower = row_at < col_at, row_at > col_at

    def diagonal(g, high, low):
        value = high + (low + low.T)
        second = value[T:, T:]
        part[2 * g] = jnp.where(lower, second, value[:T, :T])
        part[2 * g + 1] = value[:T, T:]
        dv[0, pl.ds(g, 1), :] = jnp.sum(jnp.where(on_diag, second, 0.0), axis=0, keepdims=True)

    def swap_d():
        return pltpu.make_async_remote_copy(
            dv.at[0], dv.at[1], d_sem.at[0], d_sem.at[1], device_id=sibling, device_id_type=MESH
        )

    def cross_d():
        return pltpu.make_async_remote_copy(
            dv.at[2], dv.at[3], d_sem.at[2], d_sem.at[3], device_id=across, device_id_type=MESH
        )

    dv[0] = jnp.zeros_like(dv[0])
    diagonal(0, first_high, first_low)
    peers = 2 + has_right.astype(jnp.int32) + has_left.astype(jnp.int32)
    pl.semaphore_wait(barrier, peers)
    swap(0).start()
    diagonal(1, dot(bt[hi, :], bh[:, hi]), dot(bt[hi, :], bl[:, hi]))
    swap(1).start()
    swap_d().start()
    send_on(0)
    off = dot(bt[lo, :], bh[:, hi]) + (dot(bt[lo, :], bl[:, hi]) + dot(bt[hi, :], bl[:, lo]).T)
    for k in range(4, 8):
        i, j = BLOCKS[k]
        part[k] = off[i * T : i * T + T, (j - 2) * T : (j - 1) * T]
    swap(2).start()
    swap(3).start()
    swap_d().wait_recv()
    dv[2] = dv[0] + dv[1]
    cross_d().start()
    for g in (1, 2, 3):
        send_on(g)

    def summed(g):
        cross(g).wait_recv()
        group = pl.ds(*GROUPS[g])
        fin[group, mine] = part[group, mine] + recv_b[group]
        share(g, mine).start()

    cycle = 2 * pair_count - 1
    now = round_ref[0]

    def wrap(value):
        return lax.rem(lax.rem(value, cycle) + cycle, cycle)

    top_id = jnp.where(pos == 0, 0, 1 + wrap(pos - 1 - now))
    bottom_id = 1 + wrap(2 * pair_count - 2 - pos - now)
    sign = jnp.where(top_id < bottom_id, 1.0, -1.0).astype(F32)
    along, down = [None] * 4, [None] * 4

    def diag_from(i, row):
        spread = jnp.where(on_diag, row, 0.0)
        along[i] = jnp.sum(spread, axis=0, keepdims=True)
        down[i] = jnp.sum(spread, axis=1, keepdims=True)

    total = jnp.zeros((T, T), F32)
    summed(0)
    cross_d().wait_recv()
    d_last = dv[2] + dv[3]
    for g in range(len(GROUPS)):
        if g + 1 < len(GROUPS):
            summed(g + 1)
        share(g, other).wait_recv()
        first, count = GROUPS[g]
        for k in range(first, first + count):
            i, j = BLOCKS[k]
            value = fin[k]
            if i == j:
                diag_from(i, value)
                diag_from(i + 1, d_last[g : g + 1, :])
                for m, keep in ((i, upper), (i + 1, lower)):
                    s = value / (down[m] + along[m] + EPS)
                    s = jnp.where(keep, s, 0.0)
                    if m > i:
                        s = -s
                    total = total + 2.0 * (s * s)
                    at = pl.ds(m * T, T)
                    x[at, at] = s - s.T
            else:
                si, sj = pl.ds(i * T, T), pl.ds(j * T, T)
                s = value / (down[i] + along[j] + EPS)
                if i < 2 <= j:
                    s = s * sign
                total = total + 2.0 * (s * s)
                x[si, sj] = s
                x[sj, si] = -s.T
    scale = 1.0 / jnp.sqrt(1.0 + jnp.sum(total, keepdims=True))
    wide_eye = (
        lax.broadcasted_iota(jnp.int32, (cols, cols), 0)
        == lax.broadcasted_iota(jnp.int32, (cols, cols), 1)
    )
    start = (x[...] + jnp.where(wide_eye, 1.0, 0.0)) * scale
    x[...] = start
    h, l = split(start)
    xh[...] = h
    xl[...] = l

    def put(r, c, value):
        h, l = split(value)
        ph[r, c] = h
        pm[r, c] = l

    narrow_eye = jnp.where(
        lax.broadcasted_iota(jnp.int32, (width, width), 0)
        == lax.broadcasted_iota(jnp.int32, (width, width), 1),
        1.5,
        0.0,
    )
    for step in range(STEPS):
        cross_part = dot_nt(xh[lo, :], xh[hi, :]) + (
            dot_nt(xh[lo, :], xl[hi, :]) + dot_nt(xl[lo, :], xh[hi, :])
        )
        cross_part = -0.5 * cross_part
        put(lo, hi, cross_part)
        put(hi, lo, cross_part.T)
        for r in (lo, hi):
            m = dot_nt(xh[r, :], xl[r, :])
            put(r, r, narrow_eye - 0.5 * (dot_nt(xh[r, :], xh[r, :]) + (m + m.T)))
        new = dot(xh[...], ph[...]) + (dot(xh[...], pm[...]) + dot(xl[...], ph[...]))
        h, l = split(new)
        xh[...] = h
        xl[...] = l

    @pl.when(pos == 0)
    def _():
        ph[:, :width] = xh[:, width:]
        ph[:, width:] = xh[:, :width]
        pm[:, :width] = xl[:, width:]
        pm[:, width:] = xl[:, :width]

    @pl.when(pos > 0)
    def _():
        ph[...] = xh[...]
        pm[...] = xl[...]

    def to_right(i):
        rs = pl.ds(i * step_rows, step_rows)
        return pltpu.make_async_remote_copy(
            out_r.at[rs], top.at[rs], r_send.at[i], r_recv.at[i],
            device_id=right, device_id_type=MESH,
        )

    def to_left(i):
        rs = pl.ds(i * step_rows, step_rows)
        return pltpu.make_async_remote_copy(
            out_l.at[rs], bot.at[rs], l_send.at[i], l_recv.at[i],
            device_id=left, device_id_type=MESH,
        )

    def rotate(i, carry):
        rs = pl.ds(pl.multiple_of(i * step_rows, step_rows), step_rows)
        h, l = bh[rs, :], bl[rs, :]
        r = dot(h, ph[...]) + (dot(h, pm[...]) + dot(l, ph[...]))
        out_r[rs, :] = r[:, :width]
        out_l[rs, :] = r[:, width:]

        @pl.when(has_right)
        def _():
            to_right(i).start()

        @pl.when(jnp.logical_not(has_right))
        def _():
            pltpu.make_async_copy(out_r.at[rs], bot.at[rs], l_recv.at[i]).start()

        @pl.when(has_left)
        def _():
            to_left(i).start()

        @pl.when(jnp.logical_not(has_left))
        def _():
            pltpu.make_async_copy(out_l.at[rs], top.at[rs], r_recv.at[i]).start()

        return carry

    lax.fori_loop(0, CHUNKS, rotate, 0)

    for g in range(len(GROUPS)):
        swap(g).wait_send()
        cross(g).wait_send()
        share(g, mine).wait_send()
    swap_d().wait_send()
    cross_d().wait_send()

    def finish(i, carry):
        @pl.when(has_right)
        def _():
            to_right(i).wait_send()

        @pl.when(has_left)
        def _():
            to_left(i).wait_send()

        to_right(i).wait_recv()
        to_left(i).wait_recv()
        return carry

    lax.fori_loop(0, CHUNKS, finish, 0)


def join(top, bot, out, sem):
    rows, width = top.shape
    copies = []
    for k in range(PIECES):
        rs = pl.ds(k * rows // PIECES, rows // PIECES)
        for i, half in enumerate((top, bot)):
            copies.append(
                pltpu.make_async_copy(
                    half.at[rs], out.at[rs, pl.ds(i * width, width)], sem.at[i, k]
                )
            )
    for copy in copies:
        copy.start()
    for copy in copies:
        copy.wait()


def shards(history, round_index):
    rows, cols = history.shape
    width = cols // 2
    vmem = pltpu.VMEM
    dma = pltpu.SemaphoreType.DMA
    top, bot = pl.pallas_call(
        kernel,
        out_shape=[jax.ShapeDtypeStruct((rows, width), F32)] * 2,
        in_specs=[
            pl.BlockSpec(memory_space=pltpu.SMEM),
            pl.BlockSpec(memory_space=pl.ANY),
        ],
        out_specs=[pl.BlockSpec(memory_space=pl.ANY)] * 2,
        scratch_shapes=[
            vmem((rows, cols), F32),
            vmem((rows, cols), BF16),
            vmem((rows, cols), BF16),
            vmem((cols, rows), BF16),
            vmem((len(BLOCKS), T, T), F32),
            vmem((len(BLOCKS), T, T), F32),
            vmem((len(BLOCKS), T // 2, T), F32),
            vmem((len(BLOCKS), T // 2, T), F32),
            vmem((4, 8, T), F32),
            vmem((cols, cols), F32),
            vmem((cols, cols), BF16),
            vmem((cols, cols), BF16),
            vmem((cols, cols), BF16),
            vmem((cols, cols), BF16),
            vmem((rows, width), F32),
            vmem((rows, width), F32),
            dma((CHUNKS,)),
            dma((2, len(GROUPS))),
            dma((2, len(GROUPS))),
            dma((2, len(GROUPS))),
            dma((4,)),
            dma((CHUNKS,)),
            dma((CHUNKS,)),
            dma((CHUNKS,)),
            dma((CHUNKS,)),
        ],
        compiler_params=pltpu.CompilerParams(
            collective_id=0, has_side_effects=True, vmem_limit_bytes=48 * 1024 * 1024
        ),
        name="pairing_round",
    )(round_index, history)
    return pl.pallas_call(
        join,
        out_shape=jax.ShapeDtypeStruct((rows, cols), F32),
        in_specs=[pl.BlockSpec(memory_space=pltpu.VMEM)] * 2,
        out_specs=pl.BlockSpec(memory_space=pl.ANY),
        scratch_shapes=[dma((2, PIECES))],
        compiler_params=pltpu.CompilerParams(vmem_limit_bytes=8 * 1024 * 1024),
        name="join",
    )(top, bot)


def solution(mesh):
    in_specs = (P("tm", "pair"), P())
    out_specs = P("tm", "pair")
    return jax.shard_map(shards, mesh=mesh, in_specs=in_specs, out_specs=out_specs, check_vma=False)
```

time: 85.1 us -> 78.9 us (0.927)
  Pallas kernels: 81.7 us -> 78.2 us
  other arithmetic: 2.67 us -> 0 us
    pallas_call x1, Pallas kernels: 81.7 us -> 76.1 us  [shards(): pl.pallas_call(kernel, out_shape=[jax.ShapeDtypeStruct((rows, width), F32...]
    concatenate x1 -> x0, other arithmetic: 2.67 us -> none  [shards(): return jnp.concatenate([top, bot], axis=1)]
    pallas_call x0 -> x1, Pallas kernels: none -> 2.07 us  [shards(): pl.pallas_call(join, out_shape=jax.ShapeDtypeStruct((rows, cols), F32), i...]
where the time goes in v1:
time: 78.9 us; the launch traced here: 78.8 us
  Pallas kernels  78.2 us (99%)
    pallas_call x1, Pallas kernels, shards(): pl.pallas_call(kernel, out_shape=[jax.ShapeDtypeStruct((rows, width), F32...  76.1 us
    pallas_call x1, Pallas kernels, shards(): pl.pallas_call(join, out_shape=jax.ShapeDtypeStruct((rows, cols), F32), i...  2.07 us

profile of v1, /device:TPU:7, one launch (start us, length us, event | category | flops | bytes accessed | tf_op | source)
XLA Modules:
  0.0 78.8 jit_solution(6912906473471323503)
XLA Ops:
  0.7 76.1 %pairing_round.1 = (f32[2048,256]{1,0:T(8,128)S(1)}, f32[2048,256]{1,0:T(8,128)S(1)}) custom-call(s32[1]{0:T(128)S(6)} %copy.3.round_ref, f32[2048,512]{1,0:T(8,128)} %hist.1), custom_call_target="tpu_custom_call" | custom-call | tf_op jit(solution)/shard_map/pairing_round/pallas_call | solution.py:347
  76.8 2.1 %join.1 = f32[2048,512]{1,0:T(8,128)} custom-call(f32[2048,256]{1,0:T(8,128)S(1)} %get-tuple-element.7.top, f32[2048,256]{1,0:T(8,128)S(1)} %get-tuple-element.8.bot), custom_call_target="tpu_custom_call" | custom-call | tf_op jit(solution)/shard_map/join/pallas_call | solution.py:387

commit v2 on v1

v2 whole, which is shorter than its diff:
```python
import functools

import jax
import jax.numpy as jnp
from jax import lax
from jax.experimental import pallas as pl
from jax.experimental.pallas import tpu as pltpu
from jax.sharding import PartitionSpec as P

STEPS = 4
EPS = 1e-06
T = 128
BLOCKS = [(0, 0), (0, 1), (2, 2), (2, 3), (0, 2), (0, 3), (1, 2), (1, 3)]
GROUPS = [(0, 2), (2, 2), (4, 2), (6, 2)]
DIRECT = 1
CHUNKS = 8
LOADS = 4
PIECES = 4
MESH = pl.DeviceIdType.MESH
F32 = jnp.float32
BF16 = jnp.bfloat16


def split(value):
    high = value.astype(BF16)
    return high, (value - high.astype(F32)).astype(BF16)


def dot(a, b):
    return jnp.dot(a, b, preferred_element_type=F32)


def dot_nt(a, b):
    return lax.dot_general(a, b, (((1,), (1,)), ((), ())), preferred_element_type=F32)


def kernel(
    round_ref, hist, top, bot,
    stage, bh, bl, bt, part, fin, recv_a, recv_b, recv_0, dv, xh, xl, ph, pm, out_r, out_l,
    load_sem, a_sem, b_sem, o_sem, c_sem, d_sem, r_send, l_send, r_recv, l_recv,
):
    rows, cols = hist.shape
    width = cols // 2
    step_rows = rows // CHUNKS
    load_rows = rows // LOADS
    pair_count = lax.axis_size("pair")
    pos = lax.axis_index("pair")
    tm = lax.axis_index("tm")
    core = lax.rem(tm, 2)
    sibling = {"tm": tm + 1 - 2 * core}
    across = {"tm": lax.rem(tm + 2, 4)}
    opposite = {"tm": 3 - tm}
    right = {"pair": jnp.minimum(pos + 1, pair_count - 1)}
    left = {"pair": jnp.maximum(pos - 1, 0)}
    has_right = pos < pair_count - 1
    has_left = pos > 0

    def load(i):
        rs = pl.ds(i * load_rows, load_rows)
        return pltpu.make_async_copy(hist.at[rs], stage.at[rs], load_sem.at[i])

    for i in range(LOADS):
        load(i).start()

    barrier = pltpu.get_barrier_semaphore()
    for target in (sibling, across, opposite):
        pl.semaphore_signal(barrier, inc=1, device_id=target, device_id_type=MESH)

    @pl.when(has_right)
    def _():
        pl.semaphore_signal(barrier, inc=1, device_id=right, device_id_type=MESH)

    @pl.when(has_left)
    def _():
        pl.semaphore_signal(barrier, inc=1, device_id=left, device_id_type=MESH)

    lo, hi = pl.ds(0, width), pl.ds(width, width)
    first_high, first_low = None, None
    for i in range(LOADS):
        load(i).wait()
        rs = pl.ds(i * load_rows, load_rows)
        h, l = split(stage[rs, :])
        bh[rs, :] = h
        bl[rs, :] = l
        bt[:, rs] = h.T
        new_high = dot(bt[lo, rs], bh[rs, lo])
        new_low = dot(bt[lo, rs], bl[rs, lo])
        first_high = new_high if i == 0 else first_high + new_high
        first_low = new_low if i == 0 else first_low + new_low

    mine, other = core, 1 - core

    def swap(g):
        group = pl.ds(*GROUPS[g])
        return pltpu.make_async_remote_copy(
            part.at[other, group], recv_a.at[group], a_sem.at[0, g], a_sem.at[1, g],
            device_id=sibling, device_id_type=MESH,
        )

    def straight(k):
        return pltpu.make_async_remote_copy(
            part.at[(mine, other)[k], 0], recv_0.at[k], o_sem.at[0, k], o_sem.at[1, k],
            device_id=(across, opposite)[k], device_id_type=MESH,
        )

    def crossing(g):
        first, count = GROUPS[g]
        return pl.ds(max(first, DIRECT), first + count - max(first, DIRECT))

    def cross(g):
        group = crossing(g)
        return pltpu.make_async_remote_copy(
            part.at[mine, group], recv_b.at[group], b_sem.at[0, g], b_sem.at[1, g],
            device_id=across, device_id_type=MESH,
        )

    def share(g, half):
        group = pl.ds(*GROUPS[g])
        return pltpu.make_async_remote_copy(
            fin.at[half, group], fin.at[half, group], c_sem.at[0, g], c_sem.at[1, g],
            device_id=sibling, device_id_type=MESH,
        )

    def send_on(g):
        swap(g).wait_recv()
        group = crossing(g)
        part[mine, group] = part[mine, group] + recv_a[group]
        cross(g).start()

    row_at = lax.broadcasted_iota(jnp.int32, (T, T), 0)
    col_at = lax.broadcasted_iota(jnp.int32, (T, T), 1)
    on_diag = row_at == col_at
    upper, lower = row_at < col_at, row_at > col_at

    def keep(k, value):
        part[0, k] = value[: T // 2]
        part[1, k] = value[T // 2 :]

    def diagonal(g, high, low):
        value = high + (low + low.T)
        second = value[T:, T:]
        keep(2 * g, jnp.where(lower, second, value[:T, :T]))
        keep(2 * g + 1, value[:T, T:])
        dv[0, pl.ds(g, 1), :] = jnp.sum(jnp.where(on_diag, second, 0.0), axis=0, keepdims=True)

    def send_d(k):
        return pltpu.make_async_remote_copy(
            dv.at[0], dv.at[1 + k], d_sem.at[0, k], d_sem.at[1, k],
            device_id=(sibling, across, opposite)[k], device_id_type=MESH,
        )

    dv[0] = jnp.zeros_like(dv[0])
    diagonal(0, first_high, first_low)
    peers = 3 + has_right.astype(jnp.int32) + has_left.astype(jnp.int32)
    pl.semaphore_wait(barrier, peers)
    for k in range(2):
        straight(k).start()
    swap(0).start()
    diagonal(1, dot(bt[hi, :], bh[:, hi]), dot(bt[hi, :], bl[:, hi]))
    swap(1).start()
    for k in range(3):
        send_d(k).start()
    send_on(0)
    off = dot(bt[lo, :], bh[:, hi]) + (dot(bt[lo, :], bl[:, hi]) + dot(bt[hi, :], bl[:, lo]).T)
    for k in range(4, 8):
        i, j = BLOCKS[k]
        keep(k, off[i * T : i * T + T, (j - 2) * T : (j - 1) * T])
    swap(2).start()
    swap(3).start()
    for g in (1, 2, 3):
        send_on(g)

    def summed(g):
        if g == 0:
            for k in range(2):
                straight(k).wait_recv()
            fin[mine, 0] = (part[mine, 0] + recv_a[0]) + (recv_0[0] + recv_0[1])
        cross(g).wait_recv()
        group = crossing(g)
        fin[mine, group] = part[mine, group] + recv_b[group]
        share(g, mine).start()

    cycle = 2 * pair_count - 1
    now = round_ref[0]

    def wrap(value):
        return lax.rem(lax.rem(value, cycle) + cycle, cycle)

    top_id = jnp.where(pos == 0, 0, 1 + wrap(pos - 1 - now))
    bottom_id = 1 + wrap(2 * pair_count - 2 - pos - now)
    sign = jnp.where(top_id < bottom_id, 1.0, -1.0).astype(F32)
    along, down = [None] * 4, [None] * 4

    def diag_from(i, row):
        spread = jnp.where(on_diag, row, 0.0)
        along[i] = jnp.sum(spread, axis=0, keepdims=True)
        down[i] = jnp.sum(spread, axis=1, keepdims=True)

    def place(r, c, value):
        h, l = split(value)
        xh[r, c] = h
        xl[r, c] = l

    total = jnp.zeros((T, T), F32)
    summed(0)
    for k in range(3):
        send_d(k).wait_recv()
    d_last = (dv[0] + dv[1]) + (dv[2] + dv[3])
    for g in range(len(GROUPS)):
        if g + 1 < len(GROUPS):
            summed(g + 1)
        share(g, other).wait_recv()
        first, count = GROUPS[g]
        for k in range(first, first + count):
            i, j = BLOCKS[k]
            value = jnp.concatenate([fin[0, k], fin[1, k]], axis=0)
            if i == j:
                diag_from(i, value)
                diag_from(i + 1, d_last[g : g + 1, :])
                for m, side in ((i, upper), (i + 1, lower)):
                    s = value / (down[m] + along[m] + EPS)
                    s = jnp.where(side, s, 0.0)
                    if m > i:
                        s = -s
                    total = total + 2.0 * (s * s)
                    at = pl.ds(m * T, T)
                    place(at, at, s - s.T)
            else:
                si, sj = pl.ds(i * T, T), pl.ds(j * T, T)
                s = value / (down[i] + along[j] + EPS)
                if i < 2 <= j:
                    s = s * sign
                total = total + 2.0 * (s * s)
                place(si, sj, s)
                place(sj, si, -s.T)
    norm = 1.0 + jnp.sum(total, keepdims=True)
    scale = 1.0 / jnp.sqrt(norm)
    scale_sq = 1.0 / norm

    def put(r, c, value):
        h, l = split(value)
        ph[r, c] = h
        pm[r, c] = l

    def eye(size):
        return lax.broadcasted_iota(jnp.int32, (size, size), 0) == lax.broadcasted_iota(
            jnp.int32, (size, size), 1
        )

    narrow_eye = eye(width)
    for step in range(STEPS):
        weight = -0.5 * scale_sq if step == 0 else -0.5
        on = 1.5 - 0.5 * scale_sq if step == 0 else 1.5
        cross_part = dot_nt(xh[lo, :], xh[hi, :]) + (
            dot_nt(xh[lo, :], xl[hi, :]) + dot_nt(xl[lo, :], xh[hi, :])
        )
        cross_part = weight * cross_part
        put(lo, hi, cross_part)
        put(hi, lo, cross_part.T)
        for r in (lo, hi):
            m = dot_nt(xh[r, :], xl[r, :])
            square = dot_nt(xh[r, :], xh[r, :]) + (m + m.T)
            put(r, r, jnp.where(narrow_eye, on, 0.0) + weight * square)
        new = None
        for c in (lo, hi):
            more = dot(xh[:, c], ph[c, :]) + (dot(xl[:, c], ph[c, :]) + dot(xh[:, c], pm[c, :]))
            new = more if new is None else new + more
        if step == 0:
            new = scale * (new + (ph[...].astype(F32) + pm[...].astype(F32)))
        h, l = split(new)
        xh[...] = h
        xl[...] = l

    def to_right(i, source=out_r):
        rs = pl.ds(i * step_rows, step_rows)
        return pltpu.make_async_remote_copy(
            source.at[rs], top.at[rs], r_send.at[i], r_recv.at[i],
            device_id=right, device_id_type=MESH,
        )

    def to_left(i):
        rs = pl.ds(i * step_rows, step_rows)
        return pltpu.make_async_remote_copy(
            out_l.at[rs], bot.at[rs], l_send.at[i], l_recv.at[i],
            device_id=left, device_id_type=MESH,
        )

    def rotated(i, columns):
        rs = pl.ds(pl.multiple_of(i * step_rows, step_rows), step_rows)
        h, l = bh[rs, :], bl[rs, :]
        w_h, w_l = xh[:, columns], xl[:, columns]
        return rs, dot(h, w_h) + (dot(h, w_l) + dot(l, w_h))

    def rotate_top(i, carry):
        rs, r = rotated(i, lo)
        out_r[rs, :] = r

        @pl.when(jnp.logical_and(has_left, has_right))
        def _():
            to_right(i).start()

        @pl.when(jnp.logical_not(has_right))
        def _():
            pltpu.make_async_copy(out_r.at[rs], bot.at[rs], l_recv.at[i]).start()

        @pl.when(jnp.logical_not(has_left))
        def _():
            pltpu.make_async_copy(out_r.at[rs], top.at[rs], r_recv.at[i]).start()

        return carry

    lax.fori_loop(0, CHUNKS, rotate_top, 0)

    def rotate_bottom(i, carry):
        rs, r = rotated(i, hi)
        out_l[rs, :] = r

        @pl.when(has_left)
        def _():
            to_left(i).start()

        @pl.when(jnp.logical_not(has_left))
        def _():
            to_right(i, out_l).start()

        return carry

    lax.fori_loop(0, CHUNKS, rotate_bottom, 0)

    for g in range(len(GROUPS)):
        swap(g).wait_send()
        cross(g).wait_send()
        share(g, mine).wait_send()
    for k in range(2):
        straight(k).wait_send()
    for k in range(3):
        send_d(k).wait_send()

    def finish(i, carry):
        @pl.when(has_right)
        def _():
            to_right(i).wait_send()

        @pl.when(has_left)
        def _():
            to_left(i).wait_send()

        to_right(i).wait_recv()
        to_left(i).wait_recv()
        return carry

    lax.fori_loop(0, CHUNKS, finish, 0)


def join(top, bot, out, sem):
    rows, width = top.shape
    copies = []
    for k in range(PIECES):
        rs = pl.ds(k * rows // PIECES, rows // PIECES)
        for i, half in enumerate((top, bot)):
            copies.append(
                pltpu.make_async_copy(
                    half.at[rs], out.at[rs, pl.ds(i * width, width)], sem.at[i, k]
                )
            )
    for copy in copies:
        copy.start()
    for copy in copies:
        copy.wait()


def shards(history, round_index):
    rows, cols = history.shape
    width = cols // 2
    vmem = pltpu.VMEM
    dma = pltpu.SemaphoreType.DMA
    top, bot = pl.pallas_call(
        kernel,
        out_shape=[jax.ShapeDtypeStruct((rows, width), F32)] * 2,
        in_specs=[
            pl.BlockSpec(memory_space=pltpu.SMEM),
            pl.BlockSpec(memory_space=pl.ANY),
        ],
        out_specs=[pl.BlockSpec(memory_space=pl.ANY)] * 2,
        scratch_shapes=[
            vmem((rows, cols), F32),
            vmem((rows, cols), BF16),
            vmem((rows, cols), BF16),
            vmem((cols, rows), BF16),
            vmem((2, len(BLOCKS), T // 2, T), F32),
            vmem((2, len(BLOCKS), T // 2, T), F32),
            vmem((len(BLOCKS), T // 2, T), F32),
            vmem((len(BLOCKS), T // 2, T), F32),
            vmem((2, T // 2, T), F32),
            vmem((4, 8, T), F32),
            vmem((cols, cols), BF16),
            vmem((cols, cols), BF16),
            vmem((cols, cols), BF16),
            vmem((cols, cols), BF16),
            vmem((rows, width), F32),
            vmem((rows, width), F32),
            dma((LOADS,)),
            dma((2, len(GROUPS))),
            dma((2, len(GROUPS))),
            dma((2, 2)),
            dma((2, len(GROUPS))),
            dma((2, 3)),
            dma((CHUNKS,)),
            dma((CHUNKS,)),
            dma((CHUNKS,)),
            dma((CHUNKS,)),
        ],
        compiler_params=pltpu.CompilerParams(
            collective_id=0, has_side_effects=True, vmem_limit_bytes=48 * 1024 * 1024
        ),
        name="pairing_round",
    )(round_index, history)
    return pl.pallas_call(
        join,
        out_shape=jax.ShapeDtypeStruct((rows, cols), F32),
        in_specs=[pl.BlockSpec(memory_space=pltpu.VMEM)] * 2,
        out_specs=pl.BlockSpec(memory_space=pl.ANY),
        scratch_shapes=[dma((2, PIECES))],
        compiler_params=pltpu.CompilerParams(vmem_limit_bytes=8 * 1024 * 1024),
        name="join",
    )(top, bot)


def solution(mesh):
    in_specs = (P("tm", "pair"), P())
    out_specs = P("tm", "pair")
    return jax.shard_map(shards, mesh=mesh, in_specs=in_specs, out_specs=out_specs, check_vma=False)
```

time: 78.9 us -> 78 us (0.989)
  Pallas kernels: 78.2 us -> 77.3 us
    pallas_call x1, Pallas kernels: 76.1 us -> 75.2 us  [shards(): pl.pallas_call(kernel, out_shape=[jax.ShapeDtypeStruct((rows, width), F32...]
where the time goes in v2:
time: 78 us; the launch traced here: 77.9 us
  Pallas kernels  77.3 us (99%)
    pallas_call x1, Pallas kernels, shards(): pl.pallas_call(kernel, out_shape=[jax.ShapeDtypeStruct((rows, width), F32...  75.2 us
    pallas_call x1, Pallas kernels, shards(): pl.pallas_call(join, out_shape=jax.ShapeDtypeStruct((rows, cols), F32), i...  2.07 us

profile of v2, /device:TPU:7, one launch (start us, length us, event | category | flops | bytes accessed | tf_op | source)
XLA Modules:
  0.0 77.9 jit_solution(6432379805650156428)
XLA Ops:
  0.7 75.2 %pairing_round.1 = (f32[2048,256]{1,0:T(8,128)S(1)}, f32[2048,256]{1,0:T(8,128)S(1)}) custom-call(s32[1]{0:T(128)S(6)} %copy.3.round_ref, f32[2048,512]{1,0:T(8,128)} %hist.1), custom_call_target="tpu_custom_call" | custom-call | tf_op jit(solution)/shard_map/pairing_round/pallas_call | solution.py:377
  75.9 2.1 %join.1 = f32[2048,512]{1,0:T(8,128)} custom-call(f32[2048,256]{1,0:T(8,128)S(1)} %get-tuple-element.7.top, f32[2048,256]{1,0:T(8,128)S(1)} %get-tuple-element.8.bot), custom_call_target="tpu_custom_call" | custom-call | tf_op jit(solution)/shard_map/join/pallas_call | solution.py:418

commit v3 on v2

--- a/solution.py
+++ b/solution.py
@@ -11,7 +11,7 @@
 EPS = 1e-06
 T = 128
 BLOCKS = [(0, 0), (0, 1), (2, 2), (2, 3), (0, 2), (0, 3), (1, 2), (1, 3)]
-GROUPS = [(0, 2), (2, 2), (4, 2), (6, 2)]
+GROUPS = [(0, 2), (2, 2), (4, 3), (7, 1)]
 DIRECT = 1
 CHUNKS = 8
 LOADS = 4
@@ -167,7 +167,7 @@
         keep(k, off[i * T : i * T + T, (j - 2) * T : (j - 1) * T])
     swap(2).start()
     swap(3).start()
-    for g in (1, 2, 3):
+    for g in range(1, 4):
         send_on(g)
 
     def summed(g):
@@ -261,10 +261,22 @@
             m = dot_nt(xh[r, :], xl[r, :])
             square = dot_nt(xh[r, :], xh[r, :]) + (m + m.T)
             put(r, r, jnp.where(narrow_eye, on, 0.0) + weight * square)
-        new = None
-        for c in (lo, hi):
-            more = dot(xh[:, c], ph[c, :]) + (dot(xl[:, c], ph[c, :]) + dot(xh[:, c], pm[c, :]))
-            new = more if new is None else new + more
+        if step == 0:
+            upper_part = dot(xh[lo, :], ph[...]) + (
+                dot(xl[lo, :], ph[...]) + dot(xh[lo, :], pm[...])
+            )
+            last = dot(xh[hi, :], ph[:, hi]) + (
+                dot(xl[hi, :], ph[:, hi]) + dot(xh[hi, :], pm[:, hi])
+            )
+            lower_part = jnp.concatenate([-upper_part[:, width:].T, last], axis=1)
+            new = jnp.concatenate([upper_part, lower_part], axis=0)
+        else:
+            new = None
+            for c in (lo, hi):
+                more = dot(xh[:, c], ph[c, :]) + (
+                    dot(xl[:, c], ph[c, :]) + dot(xh[:, c], pm[c, :])
+                )
+                new = more if new is None else new + more
         if step == 0:
             new = scale * (new + (ph[...].astype(F32) + pm[...].astype(F32)))
         h, l = split(new)

time: 78 us -> 78 us (level)
  no operation moved by 1% of the time
where the time goes in v3:
time: 78 us; the launch traced here: 77.9 us
  Pallas kernels  77.2 us (99%)
    pallas_call x1, Pallas kernels, shards(): pl.pallas_call(kernel, out_shape=[jax.ShapeDtypeStruct((rows, width), F32...  75.2 us
    pallas_call x1, Pallas kernels, shards(): pl.pallas_call(join, out_shape=jax.ShapeDtypeStruct((rows, cols), F32), i...  2.07 us

profile of v3, /device:TPU:7, one launch (start us, length us, event | category | flops | bytes accessed | tf_op | source)
XLA Modules:
  0.0 77.9 jit_solution(10017321790204277170)
XLA Ops:
  0.7 75.2 %pairing_round.1 = (f32[2048,256]{1,0:T(8,128)S(1)}, f32[2048,256]{1,0:T(8,128)S(1)}) custom-call(s32[1]{0:T(128)S(6)} %copy.3.round_ref, f32[2048,512]{1,0:T(8,128)} %hist.1), custom_call_target="tpu_custom_call" | custom-call | tf_op jit(solution)/shard_map/pairing_round/pallas_call | solution.py:389
  75.8 2.1 %join.1 = f32[2048,512]{1,0:T(8,128)} custom-call(f32[2048,256]{1,0:T(8,128)S(1)} %get-tuple-element.7.top, f32[2048,256]{1,0:T(8,128)S(1)} %get-tuple-element.8.bot), custom_call_target="tpu_custom_call" | custom-call | tf_op jit(solution)/shard_map/join/pallas_call | solution.py:430
